TPU v7x, 32 devices: a whole 2x2x4 slice. The times are simulated.
32 devices in a mesh: row: 4 (over y, core), col: 8 (over z, x).
Axes of the slice: x: 2, y: 2, z: 4, core: 2. Of those that a mesh axis runs over, the one named last changes fastest.
Arguments:
- weight: bfloat16 [8192, 16384], P('row', 'col'), may hold values from -3 to 3
- momentum: float32 [8192, 16384], P('row', 'col'), may hold values from -100 to 100, as said below
- gradient: bfloat16 [8192, 16384], P('row', 'col'), may hold values from -6 to 6
- prev_basis: bfloat16 [16384, 512], P('col'), may hold values from -6 to 6
Outputs:
- new_weight: bfloat16 [8192, 16384], P('row', 'col')
- new_momentum: float32 [8192, 16384], P('row', 'col')
- new_basis: bfloat16 [16384, 512], P('col')
Inputs may be any that keep to these rules, and one draw needn't show every extreme that they name: momentum has rows and columns of different scales.
All inputs are finite; a program needn't handle non-finite values.
Results may differ from a plain program's by a relative error of at most 0.0021.
Values may be sent and summed in bfloat16 or wider, within the bound.
No kernel may reach another device: no remote copies, remote signals or barrier semaphores. Data moves between devices by JAX's collectives and lax.ppermute only.
A program may use at most 128 MiB of HBM per device.

v0:
```python
import jax
import jax.numpy as jnp
from jax import lax
from jax.sharding import PartitionSpec as P

M = 8192
N = 16384
decay_loss = 0.1
step_size = 0.4
epsilon = 1e-06


def orthogonalize(left_factor, gram_matrix):
    lower_tri = jnp.linalg.cholesky(gram_matrix)
    return jax.scipy.linalg.solve_triangular(lower_tri, left_factor.T, lower=True).T


def per_device(weight, momentum, gradient, prev_basis):
    high = lax.Precision.HIGHEST
    buffer = momentum + gradient.astype(jnp.float32)
    partial_left = jnp.dot(buffer, prev_basis.astype(jnp.float32), precision=high)
    left_factor = lax.psum(partial_left, "col")
    gram_matrix = lax.psum(jnp.dot(left_factor.T, left_factor, precision=high), "row")
    orthonormal = orthogonalize(left_factor, gram_matrix)
    right_piece = lax.psum_scatter(
        jnp.dot(buffer.T, orthonormal, precision=high), "row", scatter_dimension=0, tiled=True
    )
    square_sum = lax.psum(jnp.sum(right_piece * right_piece, axis=0), ("row", "col"))
    column_scale = jnp.sqrt(square_sum / N + epsilon)
    basis_piece = (right_piece / column_scale).astype(jnp.bfloat16)
    new_basis = lax.all_gather(basis_piece, "row", axis=0, tiled=True)
    basis_float = new_basis.astype(jnp.float32)
    new_momentum = buffer - decay_loss * jnp.dot(
        orthonormal * column_scale, basis_float.T, precision=high
    )
    update = jnp.dot(orthonormal, basis_float.T, precision=high)
    new_weight = (weight.astype(jnp.float32) - step_size * (M / N) ** 0.5 * update).astype(
        jnp.bfloat16
    )
    return (new_weight, new_momentum, new_basis)


def solution(mesh):
    return jax.shard_map(
        per_device,
        mesh=mesh,
        in_specs=(P("row", "col"), P("row", "col"), P("row", "col"), P("col", None)),
        out_specs=(P("row", "col"), P("row", "col"), P("col", None)),
        check_vma=False,
    )
```

profile of v0, /device:TPU:0, one launch (start us, length us, event | category | flops | bytes accessed | tf_op | source)
XLA Modules:
  0.0 632.8 jit_solution(8107940526218711960)
XLA Ops:
  7.2 1.5 copy-done
  8.8 18.2 %fusion.1 = f32[2048,512]{1,0:T(8,128)} fusion(bf16[2048,512]{1,0:T(8,128)(2,1)S(1)} %copy-done, f32[2048,2048]{1,0:T(8,128)} %param.5, bf16[2048,2048]{1,0:T(8,128)(2,1)} %param.6), kind=kOutput, calls=%fused_computation.6 | convolution fusion | flops 25778192384 | bytes 31457280 | tf_op jit(solution)/shard_map/dot_general | solution.py:21
  27.0 159.2 %all-reduce.4.cloned.1.call-done = f32[2048,512]{1,0:T(8,128)} async-done(((f32[2048,512]{1,0:T(8,128)}), f32[2048,512]{1,0:T(8,128)}) %all-reduce.4.cloned.1.call-update) | async-done | bytes 4194320 | tf_op jit(solution)/shard_map/psum | solution.py:22
  186.2 11.4 %fusion.42 = f32[512,512]{0,1:T(8,128)} fusion(f32[2048,512]{1,0:T(8,128)} %all-reduce.4.cloned.1.call-done), kind=kOutput, calls=%fused_computation.81 | convolution fusion | flops 6442450944 | bytes 5242880 | tf_op jit(solution)/shard_map/dot_general | solution.py:23
  197.9 35.2 %all-reduce.6.cloned.1.call-done = f32[512,512]{0,1:T(8,128)} async-done(((f32[512,512]{0,1:T(8,128)}), f32[512,512]{0,1:T(8,128)}) %all-reduce.6.cloned.1.call-update) | async-done | bytes 1048592 | tf_op jit(solution)/shard_map/psum | solution.py:23
  233.1 1.6 copy.8
  234.7 1.4 fusion.18
  236.1 11.7 %cholesky.104 = f32[128,128]{1,0:T(8,128)S(1)} custom-call(f32[128,128]{1,0:T(8,128)S(1)} %cholesky.266), custom_call_target="Cholesky" | custom-call | tf_op jit(solution)/shard_map/jit(cholesky)/cholesky | solution.py:14
  247.9 9.8 %custom-call.31 = f32[1,128,128]{1,2,0:T(8,128)S(1)} custom-call(f32[1,128,128]{2,1,0:T(8,128)S(1)} %get-tuple-element.30), custom_call_target="InvertDiagBlocksLowerTriangular" | custom-call | tf_op jit(solution)/shard_map/jit(cholesky)/cholesky | solution.py:14
  258.5 11.7 %cholesky.217 = f32[128,128]{1,0:T(8,128)S(1)} custom-call(f32[128,128]{1,0:T(8,128)S(1)} %cholesky.270), custom_call_target="Cholesky" | custom-call | tf_op jit(solution)/shard_map/jit(cholesky)/cholesky | solution.py:14
  270.2 10.2 %custom-call.32 = f32[1,128,128]{1,2,0:T(8,128)S(1)} custom-call(f32[1,128,128]{2,1,0:T(8,128)S(1)} %get-tuple-element.27), custom_call_target="InvertDiagBlocksLowerTriangular" | custom-call | tf_op jit(solution)/shard_map/jit(cholesky)/cholesky | solution.py:14
  281.1 11.7 %cholesky.238 = f32[128,128]{1,0:T(8,128)S(1)} custom-call(f32[128,128]{1,0:T(8,128)S(1)} %cholesky.275), custom_call_target="Cholesky" | custom-call | tf_op jit(solution)/shard_map/jit(cholesky)/cholesky | solution.py:14
  293.5 9.8 %custom-call.33 = f32[1,128,128]{1,2,0:T(8,128)S(1)} custom-call(f32[1,128,128]{2,1,0:T(8,128)S(1)} %get-tuple-element.24), custom_call_target="InvertDiagBlocksLowerTriangular" | custom-call | tf_op jit(solution)/shard_map/jit(cholesky)/cholesky | solution.py:14
  303.9 11.7 %cholesky.255 = f32[128,128]{1,0:T(8,128)S(1)} custom-call(f32[128,128]{1,0:T(8,128)S(1)} %convolution_subtract_fusion.4), custom_call_target="Cholesky" | custom-call | tf_op jit(solution)/shard_map/jit(cholesky)/cholesky | solution.py:14
  319.8 8.0 %while.1 = (s32[]{:T(128)}, f32[512,512]{1,0:T(8,128)S(1)}, s32[4,2]{0,1:T(2,128)S(1)}, f32[4,128,128]{2,1,0:T(8,128)S(1)}, s32[]{:T(128)}) while((s32[]{:T(128)}, f32[512,512]{1,0:T(8,128)S(1)}, s32[4,2]{0,1:T(2,128)S(1)}, f32[4,128,128]{2,1,0:T(8,128)S(1)}, s32[]{:T(128)}) %tuple.31), condition=%wide.while_cond, body=%wide.while_body.sunk | while | flops 2 | bytes 131181 | solution.py:15
  320.4 1.4 bitcast_dynamic-update-slice_fusion.2
  322.4 1.4 bitcast_dynamic-update-slice_fusion.2
  324.4 1.4 bitcast_dynamic-update-slice_fusion.2
  326.4 1.4 bitcast_dynamic-update-slice_fusion.2
  327.9 39.3 %custom-call.34 = f32[4,128,128]{1,2,0:T(8,128)S(1)} custom-call(f32[4,128,128]{2,1,0:T(8,128)S(1)} %get-tuple-element.10), custom_call_target="InvertDiagBlocksLowerTriangular" | custom-call | tf_op jit(solution)/shard_map/jit(_solve_triangular)/triangular_solve | solution.py:15
  367.2 2.4 fusion.16
  369.6 3.1 convolution_subtract_fusion.1
  373.8 5.0 convolution_subtract_fusion
  379.9 7.2 %fusion.9 = f32[128,2048]{0,1:T(8,128)S(1)} fusion(f32[128,2048]{1,0:T(8,128)S(1)} %fusion.28, f32[128,2048]{1,0:T(8,128)S(1)} %fusion.30, f32[128,2048]{1,0:T(8,128)S(1)} %fusion.16, f32[512,2048]{0,1:T(8,128)S(1)} %bitcast.57, f32[512,512]{1,0:T(8,128)} %copy-done.7), kind=kOutput, calls=%fused_computation.15 | convolution fusion | flops 1209794560 | bytes 5439488 | tf_op jit(solution)/shard_map/jit(_solve_triangular)/triangular_solve | solution.py:15
  389.2 56.3 %fusion = f32[2048,512]{1,0:T(8,128)} fusion(f32[2048,2048]{1,0:T(8,128)} %param.5, bf16[2048,2048]{1,0:T(8,128)(2,1)S(1)} %bitcast.59, f32[128,2048]{1,0:T(8,128)S(1)} %fusion.27, f32[128,2048]{1,0:T(8,128)S(1)} %fusion.28, f32[128,2048]{1,0:T(8,128)S(1)} %fusion.30, f32[128,2048]{1,0:T(8,128)S(1)} %fusion.16), kind=kOutput, calls=%fused_computation.5 | convolution fusion | flops 25781338112 | bytes 33554432 | tf_op jit(solution)/shard_map/dot_general | solution.py:26
  445.6 45.2 %reduce-scatter.2.cloned.1.call-done = f32[512,512]{1,0:T(8,128)} async-done(((f32[2048,512]{1,0:T(8,128)}), f32[512,512]{1,0:T(8,128)}) %reduce-scatter.2.cloned.1.call-update) | async-done | bytes 1048592 | tf_op jit(solution)/shard_map/reduce_scatter | solution.py:25
  490.8 1.3 multiply_reduce_fusion
  492.1 39.3 %psum.23 = f32[512]{0:T(512)S(1)} all-reduce(f32[512]{0:T(512)S(1)} %multiply_reduce_fusion), channel_id=1, replica_groups=mesh['row'=4,'col'=8] {'row','col'}, use_global_device_ids=true, to_apply=%region_12.13 | all-reduce | flops 512 | bytes 4096 | tf_op jit(solution)/shard_map/psum | solution.py:28
  531.4 2.1 divide_convert_fusion
  533.6 23.5 %all-gather.2.cloned.1.call-done = bf16[2048,512]{1,0:T(8,128)(2,1)} async-done(((bf16[512,512]{1,0:T(8,128)(2,1)}), bf16[2048,512]{1,0:T(8,128)(2,1)}) %all-gather.2.cloned.1.call-update) | async-done | bytes 2097168 | tf_op jit(solution)/shard_map/all_gather | solution.py:31
  557.1 35.6 %multiply_subtract_fusion = f32[2048,2048]{1,0:T(8,128)} fusion(bf16[2048,512]{1,0:T(8,128)(2,1)} %all-gather.2.cloned.1.call-done, f32[2048,2048]{1,0:T(8,128)} %param.5, bf16[2048,2048]{1,0:T(8,128)(2,1)} %param.6, f32[512]{0:T(512)S(1)} %add_sqrt_fusion, f32[128,2048]{1,0:T(8,128)} %copy-done.6, f32[128,2048]{1,0:T(8,128)S(1)} %fusion.28, ...), kind=kOutput, calls=%fused_computation.2 | convolution fusion | flops 25790775296 | bytes 48236544 | tf_op jit(solution)/shard_map/dot_general | solution.py:33
  592.7 32.0 %subtract_convert_fusion = bf16[2048,2048]{1,0:T(8,128)(2,1)} fusion(bf16[2048,2048]{1,0:T(8,128)(2,1)} %param.4, bf16[2048,512]{1,0:T(8,128)(2,1)} %all-gather.2.cloned.1.call-done, f32[128,2048]{1,0:T(8,128)} %copy-done.6, f32[128,2048]{1,0:T(8,128)} %copy-done.4, f32[128,2048]{1,0:T(8,128)} %copy-done.3, f32[128,2048]{1,0:T(8,128)S(1)} %fusion.16), kind=kOutput, calls=%fused_computation.3 | convolution fusion | flops 25789726720 | bytes 23068672 | tf_op jit(solution)/shard_map/dot_general | solution.py:36
  (62 shorter events, 12.8 us)
Async XLA Ops:
  7.2 1.6 copy-start
  7.2 179.1 %all-reduce.4.cloned.1.call-start = ((), (), s32[]{:S(2)}) async-start(), calls=%async_computation.1 | async-start | bytes 8388608 | tf_op jit(solution)/shard_map/psum | solution.py:22
  27.0 206.1 %all-reduce.6.cloned.1.call-start = ((), (), s32[]{:S(2)}) async-start(), calls=%async_computation.2 | async-start | bytes 2097152 | tf_op jit(solution)/shard_map/psum | solution.py:23
  197.7 293.1 %reduce-scatter.2.cloned.1.call-start = ((), (), s32[]{:S(2)}) async-start(), calls=%async_computation.3 | async-start | bytes 5242880 | tf_op jit(solution)/shard_map/reduce_scatter | solution.py:25
  327.8 39.3 %copy-start.7 = (f32[512,512]{1,0:T(8,128)}, f32[512,512]{1,0:T(8,128)S(1)}, u32[]{:S(2)}) copy-start(f32[512,512]{1,0:T(8,128)S(1)} %get-tuple-element.99) | copy-start | bytes 3145732
  367.2 6.6 %copy-start.2 = (f32[2048,512]{1,0:T(8,128)S(1)}, f32[2048,512]{1,0:T(8,128)}, u32[]{:S(2)}) copy-start(f32[2048,512]{1,0:T(8,128)} %all-reduce.4.cloned.1.call-done) | copy-start | bytes 12582916
  372.7 16.5 %slice-start = ((s8[8388608]{0:T(1024)(128)(4,1)}), s8[4194304]{0:T(1024)(128)(4,1)S(1)}, s32[]{:S(2)}) async-start(s8[8388608]{0:T(1024)(128)(4,1)} %bitcast.58), calls=%async_computation.5 | async-start | bytes 8388608
  373.8 183.2 %copy-start.3 = (f32[128,2048]{1,0:T(8,128)}, f32[128,2048]{1,0:T(8,128)S(1)}, u32[]{:S(2)}) copy-start(f32[128,2048]{1,0:T(8,128)S(1)} %fusion.30) | copy-start | bytes 3145732
  378.8 10.4 %slice-start.1 = ((s8[8388608]{0:T(1024)(128)(4,1)}), s8[4194304]{0:T(1024)(128)(4,1)S(1)}, s32[]{:S(2)}) async-start(s8[8388608]{0:T(1024)(128)(4,1)} %bitcast.58), calls=%async_computation.6 | async-start | bytes 8388608
  379.9 177.2 %copy-start.4 = (f32[128,2048]{1,0:T(8,128)}, f32[128,2048]{1,0:T(8,128)S(1)}, u32[]{:S(2)}) copy-start(f32[128,2048]{1,0:T(8,128)S(1)} %fusion.28) | copy-start | bytes 3145732
  388.2 1.0 copy-start.6
  445.6 111.5 %all-gather.2.cloned.1.call-start = ((), (), s32[]{:S(2)}) async-start(), calls=%async_computation.4 | async-start | bytes 2621440 | tf_op jit(solution)/shard_map/all_gather | solution.py:31
  592.7 32.1 %copy-start.5 = (bf16[2048,512]{1,0:T(8,128)(2,1)S(1)}, bf16[2048,512]{1,0:T(8,128)(2,1)}, u32[]{:S(2)}) copy-start(bf16[2048,512]{1,0:T(8,128)(2,1)} %all-gather.2.cloned.1.call-done) | copy-start | bytes 6291460
  592.7 33.4 %copy-start.1 = (bf16[2048,512]{1,0:T(8,128)(2,1)S(1)}, bf16[2048,512]{1,0:T(8,128)(2,1)}, u32[]{:S(2)}) copy-start(bf16[2048,512]{1,0:T(8,128)(2,1)} %param.7) | copy-start | bytes 6291460
Sparse Core Ops, SparseCore 0:
  27.1 159.1 all-reduce.3
  197.8 35.2 all-reduce.5
  445.7 45.0 reduce-scatter.1
  533.7 23.3 all-gather.1
where the time goes:
time: 639 us; the launch traced here: 633 us
  waiting for transfers between devices  263 us (41%)
  matrix products  176 us (28%)
  other arithmetic  123 us (19%)
  blocking collectives  39.3 us (6%)
  between operations  16.8 us (3%)
  local copies, waits for them, and re-layouts  13.5 us (2%)
    psum x1, waiting for transfers between devices, per_device(): left_factor = lax.psum(partial_left, 'col')  159 us
    another operation x14, other arithmetic, orthogonalize(): lower_tri = jnp.linalg.cholesky(gram_matrix)  78.8 us
    dot_general x1, matrix products, per_device(): jnp.dot(buffer.T, orthonormal, precision=high)  56.3 us
    reduce_scatter x1, waiting for transfers between devices, per_device(): lax.psum_scatter(jnp.dot(buffer.T, orthonormal, precision=high), 'row', s...  45.2 us
    another operation x3, other arithmetic, orthogonalize(): jax.scipy.linalg.solve_triangular(lower_tri, left_factor.T, lower=True)  39.6 us
    psum x1, blocking collectives, per_device(): lax.psum(jnp.sum(right_piece * right_piece, axis=0), ('row', 'col'))  39.3 us
    dot_general x1, matrix products, per_device(): jnp.dot(orthonormal * column_scale, basis_float.T, precision=high)  35.6 us
    psum x1, waiting for transfers between devices, per_device(): lax.psum(jnp.dot(left_factor.T, left_factor, precision=high), 'row')  35.2 us
  transfers between devices with their start and end apart: 4, of which 4 were waited for; matrix products, arithmetic and copies ran while one was open for 0% of the time, Pallas kernels for 0%

commit v1 on v0

--- a/solution.py
+++ b/solution.py
@@ -19,7 +19,10 @@
     high = lax.Precision.HIGHEST
     buffer = momentum + gradient.astype(jnp.float32)
     partial_left = jnp.dot(buffer, prev_basis.astype(jnp.float32), precision=high)
-    left_factor = lax.psum(partial_left, "col")
+    size, left_factor = (lax.axis_size("col"), partial_left)
+    for far in [1 << k for k in range(size.bit_length() - 1)]:
+        route = [(i, i ^ far) for i in range(size)]
+        left_factor = left_factor + lax.ppermute(left_factor, "col", route)
     gram_matrix = lax.psum(jnp.dot(left_factor.T, left_factor, precision=high), "row")
     orthonormal = orthogonalize(left_factor, gram_matrix)
     right_piece = lax.psum_scatter(

time: 639 us -> 855 us (1.34)
  waiting for transfers between devices: 263 us -> 459 us
  other arithmetic: 123 us -> 134 us
    ppermute x0 -> x3, waiting for transfers between devices: none -> 360 us  [per_device(): left_factor = left_factor + lax.ppermute(left_factor, 'col', route)]
    psum x1 -> x0, waiting for transfers between devices: 159 us -> none  [per_device(): left_factor = lax.psum(partial_left, 'col')]
  transfers between devices with their start and end apart: 4 -> 6, of which waited for: 4 -> 6; matrix products, arithmetic and copies ran while one was open for 0% -> 1% of each run, Pallas kernels for 0% -> 0%
where the time goes in v1:
time: 855 us; the launch traced here: 848 us
  waiting for transfers between devices  459 us (54%)
  matrix products  176 us (21%)
  other arithmetic  134 us (16%)
  blocking collectives  39.2 us (5%)
  between operations  17 us (2%)
  local copies, waits for them, and re-layouts  14 us (2%)
    ppermute x3, waiting for transfers between devices, per_device(): left_factor = left_factor + lax.ppermute(left_factor, 'col', route)  360 us
    another operation x14, other arithmetic, orthogonalize(): lower_tri = jnp.linalg.cholesky(gram_matrix)  79 us
    dot_general x1, matrix products, per_device(): jnp.dot(buffer.T, orthonormal, precision=high)  56.3 us
    reduce_scatter x1, waiting for transfers between devices, per_device(): lax.psum_scatter(jnp.dot(buffer.T, orthonormal, precision=high), 'row', s...  45.2 us
    another operation x3, other arithmetic, orthogonalize(): jax.scipy.linalg.solve_triangular(lower_tri, left_factor.T, lower=True)  39.4 us
    psum x1, blocking collectives, per_device(): lax.psum(jnp.sum(right_piece * right_piece, axis=0), ('row', 'col'))  39.2 us
    dot_general x1, matrix products, per_device(): jnp.dot(orthonormal * column_scale, basis_float.T, precision=high)  35.6 us
    dot_general x1, matrix products, per_device(): update = jnp.dot(orthonormal, basis_float.T, precision=high)  32 us
  transfers between devices with their start and end apart: 6, of which 6 were waited for; matrix products, arithmetic and copies ran while one was open for 1% of the time, Pallas kernels for 0%

profile of v1, /device:TPU:0, one launch (start us, length us, event | category | flops | bytes accessed | tf_op | source)
XLA Modules:
  0.0 847.6 jit_solution(10008172545762618687)
XLA Ops:
  8.8 16.6 %fusion.1 = f32[2048,512]{1,0:T(8,128)S(1)} fusion(bf16[2048,512]{1,0:T(8,128)(2,1)S(1)} %copy-done, f32[2048,2048]{1,0:T(8,128)} %param.5, bf16[2048,2048]{1,0:T(8,128)(2,1)} %param.6), kind=kOutput, calls=%fused_computation.6 | convolution fusion | flops 25778192384 | bytes 31457280 | tf_op jit(solution)/shard_map/dot_general | solution.py:21
  25.4 3.0 collective-permute-start
  28.4 90.6 %collective-permute-done = f32[2048,512]{1,0:T(8,128)S(1)} collective-permute-done((f32[2048,512]{1,0:T(8,128)S(1)}, f32[2048,512]{1,0:T(8,128)S(1)}, u32[]{:S(2)}, u32[]{:S(2)}) %collective-permute-start) | collective-permute-done | bytes 4194336 | tf_op jit(solution)/shard_map/ppermute | solution.py:25
  120.0 1.9 collective-permute-start.1
  121.9 89.9 %collective-permute-done.1 = f32[2048,512]{1,0:T(8,128)S(1)} collective-permute-done((f32[2048,512]{1,0:T(8,128)S(1)}, f32[2048,512]{1,0:T(8,128)S(1)}, u32[]{:S(2)}, u32[]{:S(2)}) %collective-permute-start.1) | collective-permute-done | bytes 4194336 | tf_op jit(solution)/shard_map/ppermute | solution.py:25
  211.8 3.0 add.67
  214.8 2.6 collective-permute-start.2
  217.4 179.4 %collective-permute-done.2 = f32[2048,512]{1,0:T(8,128)} collective-permute-done((f32[2048,512]{1,0:T(8,128)}, f32[2048,512]{1,0:T(8,128)}, u32[]{:S(2)}, u32[]{:S(2)}) %collective-permute-start.2) | collective-permute-done | bytes 4194336 | tf_op jit(solution)/shard_map/ppermute | solution.py:25
  396.8 13.5 %fusion.14 = f32[512,512]{0,1:T(8,128)} fusion(f32[2048,512]{1,0:T(8,128)} %add.67, f32[2048,512]{1,0:T(8,128)} %collective-permute-done.2), kind=kOutput, calls=%fused_computation.21 | convolution fusion | flops 6443499520 | bytes 9437184 | tf_op jit(solution)/shard_map/dot_general | solution.py:26
  410.6 6.5 add_bitcast_fusion
  417.1 30.5 %all-reduce.3.cloned.1.call-done = f32[512,512]{0,1:T(8,128)} async-done(((f32[512,512]{0,1:T(8,128)}), f32[512,512]{0,1:T(8,128)}) %all-reduce.3.cloned.1.call-update) | async-done | bytes 1048592 | tf_op jit(solution)/shard_map/psum | solution.py:26
  447.6 1.6 copy.8
  450.7 11.7 %cholesky.104 = f32[128,128]{1,0:T(8,128)S(1)} custom-call(f32[128,128]{1,0:T(8,128)S(1)} %cholesky.266), custom_call_target="Cholesky" | custom-call | tf_op jit(solution)/shard_map/jit(cholesky)/cholesky | solution.py:14
  462.4 9.8 %custom-call.31 = f32[1,128,128]{1,2,0:T(8,128)S(1)} custom-call(f32[1,128,128]{2,1,0:T(8,128)S(1)} %get-tuple-element.30), custom_call_target="InvertDiagBlocksLowerTriangular" | custom-call | tf_op jit(solution)/shard_map/jit(cholesky)/cholesky | solution.py:14
  473.0 11.7 %cholesky.217 = f32[128,128]{1,0:T(8,128)S(1)} custom-call(f32[128,128]{1,0:T(8,128)S(1)} %cholesky.270), custom_call_target="Cholesky" | custom-call | tf_op jit(solution)/shard_map/jit(cholesky)/cholesky | solution.py:14
  484.8 10.3 %custom-call.32 = f32[1,128,128]{1,2,0:T(8,128)S(1)} custom-call(f32[1,128,128]{2,1,0:T(8,128)S(1)} %get-tuple-element.27), custom_call_target="InvertDiagBlocksLowerTriangular" | custom-call | tf_op jit(solution)/shard_map/jit(cholesky)/cholesky | solution.py:14
  495.7 11.7 %cholesky.238 = f32[128,128]{1,0:T(8,128)S(1)} custom-call(f32[128,128]{1,0:T(8,128)S(1)} %cholesky.275), custom_call_target="Cholesky" | custom-call | tf_op jit(solution)/shard_map/jit(cholesky)/cholesky | solution.py:14
  508.2 9.8 %custom-call.33 = f32[1,128,128]{1,2,0:T(8,128)S(1)} custom-call(f32[1,128,128]{2,1,0:T(8,128)S(1)} %get-tuple-element.24), custom_call_target="InvertDiagBlocksLowerTriangular" | custom-call | tf_op jit(solution)/shard_map/jit(cholesky)/cholesky | solution.py:14
  518.6 11.9 %cholesky.255 = f32[128,128]{1,0:T(8,128)S(1)} custom-call(f32[128,128]{1,0:T(8,128)S(1)} %convolution_subtract_fusion.2), custom_call_target="Cholesky" | custom-call | tf_op jit(solution)/shard_map/jit(cholesky)/cholesky | solution.py:14
  534.5 8.5 %while.1 = (s32[]{:T(128)}, f32[512,512]{1,0:T(8,128)S(1)}, s32[4,2]{0,1:T(2,128)S(1)}, f32[4,128,128]{2,1,0:T(8,128)S(1)}, s32[]{:T(128)}) while((s32[]{:T(128)}, f32[512,512]{1,0:T(8,128)S(1)}, s32[4,2]{0,1:T(2,128)S(1)}, f32[4,128,128]{2,1,0:T(8,128)S(1)}, s32[]{:T(128)}) %tuple.31), condition=%wide.while_cond, body=%wide.while_body.sunk | while | flops 2 | bytes 131181 | solution.py:15
  543.0 39.3 %custom-call.34 = f32[4,128,128]{1,2,0:T(8,128)S(1)} custom-call(f32[4,128,128]{2,1,0:T(8,128)S(1)} %get-tuple-element.10), custom_call_target="InvertDiagBlocksLowerTriangular" | custom-call | tf_op jit(solution)/shard_map/jit(_solve_triangular)/triangular_solve | solution.py:15
  582.3 2.4 fusion.19
  584.8 2.6 fusion.30
  588.6 4.9 fusion.9
  594.6 7.2 fusion.3
  603.9 56.3 %fusion = f32[2048,512]{1,0:T(8,128)} fusion(f32[2048,2048]{1,0:T(8,128)} %param.5, bf16[2048,2048]{1,0:T(8,128)(2,1)S(1)} %bitcast.51, f32[128,2048]{1,0:T(8,128)S(1)} %fusion.16, f32[128,2048]{1,0:T(8,128)S(1)} %fusion.17, f32[128,2048]{1,0:T(8,128)S(1)} %fusion.18, f32[128,2048]{1,0:T(8,128)S(1)} %fusion.19), kind=kOutput, calls=%fused_computation.5 | convolution fusion | flops 25781338112 | bytes 33554432 | tf_op jit(solution)/shard_map/dot_general | solution.py:29
  660.3 45.2 %reduce-scatter.2.cloned.1.call-done = f32[512,512]{1,0:T(8,128)} async-done(((f32[2048,512]{1,0:T(8,128)}), f32[512,512]{1,0:T(8,128)}) %reduce-scatter.2.cloned.1.call-update) | async-done | bytes 1048592 | tf_op jit(solution)/shard_map/reduce_scatter | solution.py:28
  706.8 39.2 %psum.15 = f32[512]{0:T(512)S(1)} all-reduce(f32[512]{0:T(512)S(1)} %multiply_reduce_fusion), channel_id=1, replica_groups=mesh['row'=4,'col'=8] {'row','col'}, use_global_device_ids=true, to_apply=%region_11.12 | all-reduce | flops 512 | bytes 4096 | tf_op jit(solution)/shard_map/psum | solution.py:31
  746.1 2.1 divide_convert_fusion
  748.2 23.4 %all-gather.2.cloned.1.call-done = bf16[2048,512]{1,0:T(8,128)(2,1)} async-done(((bf16[512,512]{1,0:T(8,128)(2,1)}), bf16[2048,512]{1,0:T(8,128)(2,1)}) %all-gather.2.cloned.1.call-update) | async-done | bytes 2097168 | tf_op jit(solution)/shard_map/all_gather | solution.py:34
  771.7 35.6 %multiply_subtract_fusion = f32[2048,2048]{1,0:T(8,128)} fusion(bf16[2048,512]{1,0:T(8,128)(2,1)} %all-gather.2.cloned.1.call-done, f32[2048,2048]{1,0:T(8,128)} %param.5, bf16[2048,2048]{1,0:T(8,128)(2,1)} %param.6, f32[512]{0:T(512)S(1)} %add_sqrt_fusion, f32[128,2048]{1,0:T(8,128)} %copy-done.6, f32[128,2048]{1,0:T(8,128)S(1)} %fusion.17, ...), kind=kOutput, calls=%fused_computation.2 | convolution fusion | flops 25790775296 | bytes 48236544 | tf_op jit(solution)/shard_map/dot_general | solution.py:36
  807.3 32.0 %subtract_convert_fusion = bf16[2048,2048]{1,0:T(8,128)(2,1)} fusion(bf16[2048,2048]{1,0:T(8,128)(2,1)} %param.4, bf16[2048,512]{1,0:T(8,128)(2,1)} %all-gather.2.cloned.1.call-done, f32[128,2048]{1,0:T(8,128)} %copy-done.6, f32[128,2048]{1,0:T(8,128)} %copy-done.4, f32[128,2048]{1,0:T(8,128)} %copy-done.2, f32[128,2048]{1,0:T(8,128)S(1)} %fusion.19), kind=kOutput, calls=%fused_computation.3 | convolution fusion | flops 25789726720 | bytes 23068672 | tf_op jit(solution)/shard_map/dot_general | solution.py:39
  (68 shorter events, 24.1 us)
Async XLA Ops:
  7.2 1.6 copy-start
  7.2 440.5 %all-reduce.3.cloned.1.call-start = ((), (), s32[]{:S(2)}) async-start(), calls=%async_computation.1 | async-start | bytes 2097152 | tf_op jit(solution)/shard_map/psum | solution.py:26
  25.4 93.6 %collective-permute-start = (f32[2048,512]{1,0:T(8,128)S(1)}, f32[2048,512]{1,0:T(8,128)S(1)}, u32[]{:S(2)}, u32[]{:S(2)}) collective-permute-start(f32[2048,512]{1,0:T(8,128)S(1)} %fusion.1), channel_id=1, source_target_pairs={{0,1},{1,0},{2,3},{3,2},{4,5},{5,4},{6,7},{7,6},{8,9},{9,8},{10,11... | collective-permute-start | bytes 12582920 | tf_op jit(solution)/shard_map/ppermute | solution.py:25
  120.0 91.8 %collective-permute-start.1 = (f32[2048,512]{1,0:T(8,128)S(1)}, f32[2048,512]{1,0:T(8,128)S(1)}, u32[]{:S(2)}, u32[]{:S(2)}) collective-permute-start(f32[2048,512]{1,0:T(8,128)S(1)} %add.66), channel_id=1, source_target_pairs={{0,2},{1,3},{2,0},{3,1},{4,6},{5,7},{6,4},{7,5},{8,10},{9,11},{10,... | collective-permute-start | bytes 12582920 | tf_op jit(solution)/shard_map/ppermute | solution.py:25
  214.8 182.0 %collective-permute-start.2 = (f32[2048,512]{1,0:T(8,128)}, f32[2048,512]{1,0:T(8,128)}, u32[]{:S(2)}, u32[]{:S(2)}) collective-permute-start(f32[2048,512]{1,0:T(8,128)} %add.67), channel_id=1, source_target_pairs={{0,4},{1,5},{2,6},{3,7},{4,0},{5,1},{6,2},{7,3},{8,12},{9,13},{10,... | collective-permute-start | bytes 12582920 | tf_op jit(solution)/shard_map/ppermute | solution.py:25
  410.4 295.1 %reduce-scatter.2.cloned.1.call-start = ((), (), s32[]{:S(2)}) async-start(), calls=%async_computation.2 | async-start | bytes 5242880 | tf_op jit(solution)/shard_map/reduce_scatter | solution.py:28
  543.0 39.3 %copy-start.7 = (f32[512,512]{1,0:T(8,128)}, f32[512,512]{1,0:T(8,128)S(1)}, u32[]{:S(2)}) copy-start(f32[512,512]{1,0:T(8,128)S(1)} %get-tuple-element.99) | copy-start | bytes 3145732
  582.3 5.1 copy-start.3
  587.4 16.5 %slice-start = ((s8[8388608]{0:T(1024)(128)(4,1)}), s8[4194304]{0:T(1024)(128)(4,1)S(1)}, s32[]{:S(2)}) async-start(s8[8388608]{0:T(1024)(128)(4,1)} %bitcast.50), calls=%async_computation.4 | async-start | bytes 8388608
  588.6 183.1 %copy-start.2 = (f32[128,2048]{1,0:T(8,128)}, f32[128,2048]{1,0:T(8,128)S(1)}, u32[]{:S(2)}) copy-start(f32[128,2048]{1,0:T(8,128)S(1)} %fusion.18) | copy-start | bytes 3145732
  593.5 10.4 %slice-start.1 = ((s8[8388608]{0:T(1024)(128)(4,1)}), s8[4194304]{0:T(1024)(128)(4,1)S(1)}, s32[]{:S(2)}) async-start(s8[8388608]{0:T(1024)(128)(4,1)} %bitcast.50), calls=%async_computation.5 | async-start | bytes 8388608
  594.6 177.1 %copy-start.4 = (f32[128,2048]{1,0:T(8,128)}, f32[128,2048]{1,0:T(8,128)S(1)}, u32[]{:S(2)}) copy-start(f32[128,2048]{1,0:T(8,128)S(1)} %fusion.17) | copy-start | bytes 3145732
  602.9 1.0 copy-start.6
  660.3 111.4 %all-gather.2.cloned.1.call-start = ((), (), s32[]{:S(2)}) async-start(), calls=%async_computation.3 | async-start | bytes 2621440 | tf_op jit(solution)/shard_map/all_gather | solution.py:34
  807.3 32.1 %copy-start.5 = (bf16[2048,512]{1,0:T(8,128)(2,1)S(1)}, bf16[2048,512]{1,0:T(8,128)(2,1)}, u32[]{:S(2)}) copy-start(bf16[2048,512]{1,0:T(8,128)(2,1)} %all-gather.2.cloned.1.call-done) | copy-start | bytes 6291460
  807.3 33.4 %copy-start.1 = (bf16[2048,512]{1,0:T(8,128)(2,1)S(1)}, bf16[2048,512]{1,0:T(8,128)(2,1)}, u32[]{:S(2)}) copy-start(bf16[2048,512]{1,0:T(8,128)(2,1)} %param.7) | copy-start | bytes 6291460
Sparse Core Ops, SparseCore 0:
  410.5 37.1 all-reduce.2
  660.4 45.0 reduce-scatter.1
  748.4 23.2 all-gather.1
